TPU v7x, 32 devices: a whole 2x2x4 slice. The times are simulated.
32 devices in a mesh: shard: 4 (over z), ctx: 4 (over x, core), tp: 2 (over y).
Axes of the slice: x: 2, y: 2, z: 4, core: 2. Of those that a mesh axis runs over, the one named last changes fastest.
Arguments:
- layer_in: bfloat16 [3072, 2048], P(('shard', 'ctx')), may hold values from -6 to 6
- w_qkv: bfloat16 [6144, 2048], P(('shard', 'ctx'), 'tp'), may hold values from -0.125 to 0.125
- w_out: bfloat16 [2048, 2048], P(('shard', 'ctx'), 'tp'), may hold values from -1.5 to 1.5
- norm_gains: bfloat16 [2048, 4], P(('shard', 'ctx')), may hold values from 0.25 to 1.75
- router: bfloat16 [2048, 16], P(('shard', 'ctx')), may hold values from -0.0625 to 0.0625
- w_gate_up: bfloat16 [16, 2048, 2, 1024], P(('shard', 'ctx'), None, None, 'tp'), may hold values from -0.125 to 0.125
- w_down: bfloat16 [16, 2048, 1024], P(('shard', 'ctx'), None, 'tp'), may hold values from -0.75 to 0.75
- routes: int32 [3072, 8], P(('shard', 'ctx')), may hold values from 0 to 15, all different within a row; in each aligned block of 192 rows (0 to 191, 192 to 383, ...) at most 120 rows name the same one
- lengths: int32 [4, 3], P('shard'), may hold values from 1 to 614, 768 in all within a row
- token_order: int32 [4, 768], P('shard'), may hold values from 0 to 767, each once within a row
- out_grad: bfloat16 [3072, 2048], P(('shard', 'ctx')), may hold values from -6 to 6
Outputs:
- output: bfloat16 [3072, 2048], P(('shard', 'ctx'))
- input_grad: float32 [3072, 2048], P(('shard', 'ctx'))
- qkv_grad: float32 [6144, 2048], P(('shard', 'ctx'), 'tp')
- out_proj_grad: float32 [2048, 2048], P(('shard', 'ctx'), 'tp')
- gains_grad: float32 [2048, 4], P(('shard', 'ctx'))
- router_grad: float32 [2048, 16], P(('shard', 'ctx'))
- gate_up_grad: float32 [16, 2048, 2, 1024], P(('shard', 'ctx'), None, None, 'tp')
- down_grad: float32 [16, 2048, 1024], P(('shard', 'ctx'), None, 'tp')
Inputs may be any that keep to these rules, and one draw needn't show every extreme that they name: `routes`: each row names 8 different experts. Among the 192 rows of one device no expert is named more than 120 times, a bound that some block reaches there. Each row holds the lengths of the 3 sequences of one group; they sum to 768 and the longest is exactly 614. `token_order`: each row is a permutation of the places of its group.
All inputs are finite; a program needn't handle non-finite values.
Results may differ from a plain program's by a relative error of at most 0.017.
Values may be sent and summed in bfloat16 or wider, within the bound.
No kernel may reach another device: no remote copies, remote signals or barrier semaphores. Data moves between devices by JAX's collectives and lax.ppermute only.
A program may use at most 320 MiB of HBM per device.

v0:
```python
import jax
import jax.numpy as jnp
from jax import lax
from jax.sharding import PartitionSpec as P

HEAD = 128


norm_eps = 1e-05
rope_base = 10000.0
masked_score = -1e30


def places_info(order_row, length_row):
    seq_ends = jnp.cumsum(length_row)
    seq_starts = seq_ends - length_row
    sequence = jnp.sum((order_row[:, None] >= seq_ends[None, :]).astype(jnp.int32), axis=1)
    picker = jnp.arange(length_row.shape[0], dtype=jnp.int32)[None, :] == sequence[:, None]
    first_place = jnp.sum(jnp.where(picker, seq_starts[None, :], 0), axis=1)
    return (sequence, order_row - first_place)


def rope_tables(place_pos, head_size):
    freq_index = jnp.arange(head_size // 2, dtype=jnp.float32)
    inverse = 1.0 / rope_base ** (freq_index * 2.0 / head_size)
    angle = place_pos.astype(jnp.float32)[:, None] * inverse[None, :]
    cosine = jnp.cos(angle)
    sine = jnp.sin(angle)
    return (jnp.concatenate([cosine, cosine], 1), jnp.concatenate([sine, sine], 1))


def rotate(values_in, cosine, sine):
    half_width = values_in.shape[-1] // 2
    turned = jnp.concatenate([-values_in[..., half_width:], values_in[..., :half_width]], -1)
    return values_in * cosine[:, None, :] + turned * sine[:, None, :]


def rotate_back(grad_in, cosine, sine):
    half_width = grad_in.shape[-1] // 2
    scaled = grad_in * sine[:, None, :]
    return grad_in * cosine[:, None, :] + jnp.concatenate(
        [scaled[..., half_width:], -scaled[..., :half_width]], -1
    )


def slot_index(expert_flat, expert_count, capacity):
    chosen = (expert_flat[:, None] == jnp.arange(expert_count, dtype=jnp.int32)[None, :]).astype(
        jnp.int32
    )
    before = jnp.cumsum(chosen, axis=0) - chosen
    slot_num = jnp.sum(before * chosen, axis=1)
    return expert_flat * capacity + slot_num


def local(
    layer_in,
    w_qkv,
    w_out,
    norm_gains,
    router,
    w_gate_up,
    w_down,
    routes,
    lengths,
    token_order,
    out_grad,
):
    tokens, width = layer_in.shape
    topk = routes.shape[1]
    experts = router.shape[1]
    capacity = max(2, tokens * topk * 5 // (4 * experts))
    qkv_all, out_all, gains_all, router_all = (
        lax.all_gather(w_qkv, ("shard", "ctx"), axis=0, tiled=True),
        lax.all_gather(w_out, ("shard", "ctx"), axis=0, tiled=True),
        lax.all_gather(norm_gains, ("shard", "ctx"), axis=0, tiled=True),
        lax.all_gather(router, ("shard", "ctx"), axis=0, tiled=True),
    )
    half_width = qkv_all.shape[1]
    full_heads = half_width * lax.axis_size("tp")
    head_count = half_width // HEAD
    tp_index = lax.axis_index("tp")
    ctx_index = lax.axis_index("ctx")
    gains_f = gains_all.astype(jnp.float32)
    gain_in = gains_f[:, 0]
    gain_mid = gains_f[:, 1]
    gain_q = lax.dynamic_slice_in_dim(gains_f[:, 2], tp_index * half_width, half_width)
    gain_k = lax.dynamic_slice_in_dim(gains_f[:, 3], tp_index * half_width, half_width)
    score_scale = HEAD ** (-0.5)
    group_len = token_order.shape[1]
    seq_all, pos_all = places_info(token_order[0], lengths[0])
    seq_mine = lax.dynamic_slice_in_dim(seq_all, ctx_index * tokens, tokens)
    pos_mine = lax.dynamic_slice_in_dim(pos_all, ctx_index * tokens, tokens)
    cosine, sine = rope_tables(pos_mine, HEAD)
    visible = (seq_mine[:, None] == seq_all[None, :]) & (pos_all[None, :] <= pos_mine[:, None])
    layer_f = layer_in.astype(jnp.float32)
    rate_in = lax.rsqrt(jnp.mean(layer_f * layer_f, axis=-1, keepdims=True) + norm_eps)
    in_hat = layer_f * rate_in
    in_norm = in_hat * gain_in
    in_low = in_norm.astype(jnp.bfloat16)
    qkv_mats = qkv_all.reshape(3, width, half_width)
    projected = jnp.einsum("td,jdh->tjh", in_low, qkv_mats, preferred_element_type=jnp.float32)
    q_raw = projected[:, 0]
    k_raw = projected[:, 1]
    v_raw = projected[:, 2]
    square_q, square_k = lax.psum(
        (jnp.sum(q_raw * q_raw, axis=1), jnp.sum(k_raw * k_raw, axis=1)), "tp"
    )
    rate_q = lax.rsqrt(square_q / full_heads + norm_eps)[:, None]
    rate_k = lax.rsqrt(square_k / full_heads + norm_eps)[:, None]
    q_hat = q_raw * rate_q
    k_hat = k_raw * rate_k
    q_low = rotate((q_hat * gain_q).reshape(tokens, head_count, HEAD), cosine, sine).astype(
        jnp.bfloat16
    )
    k_low = (
        rotate((k_hat * gain_k).reshape(tokens, head_count, HEAD), cosine, sine)
        .astype(jnp.bfloat16)
        .reshape(tokens, half_width)
    )
    v_low = v_raw.astype(jnp.bfloat16)
    key_rows, value_rows = (
        lax.all_gather(k_low, "ctx", axis=0, tiled=True),
        lax.all_gather(v_low, "ctx", axis=0, tiled=True),
    )
    key_heads = key_rows.reshape(group_len, head_count, HEAD)
    value_heads = value_rows.reshape(group_len, head_count, HEAD)
    scores = (
        jnp.einsum("qhd,khd->hqk", q_low, key_heads, preferred_element_type=jnp.float32)
        * score_scale
    )
    scores = jnp.where(visible[None], scores, masked_score)
    row_max = jnp.max(scores, axis=-1, keepdims=True)
    shifted = jnp.exp(scores - row_max)
    row_sum = jnp.sum(shifted, axis=-1, keepdims=True)
    weights = shifted / row_sum
    log_total = row_max + jnp.log(row_sum)
    mixed = jnp.einsum(
        "hqk,khd->qhd",
        weights.astype(jnp.bfloat16),
        value_heads,
        preferred_element_type=jnp.float32,
    )
    mixed_low = mixed.reshape(tokens, half_width).astype(jnp.bfloat16)
    attn_part = lax.dot_general(
        mixed_low, out_all, (((1,), (1,)), ((), ())), preferred_element_type=jnp.float32
    )
    attn = lax.psum(attn_part, "tp")
    resid = layer_f + attn
    rate_mid = lax.rsqrt(jnp.mean(resid * resid, axis=-1, keepdims=True) + norm_eps)
    mid_hat = resid * rate_mid
    mid_norm = mid_hat * gain_mid
    mid_low = mid_norm.astype(jnp.bfloat16)
    router_f = router_all.astype(jnp.float32)
    logits = jnp.dot(mid_norm, router_f, precision=lax.Precision.HIGHEST)
    chosen = routes[:, :, None] == jnp.arange(experts, dtype=jnp.int32)[None, None, :]
    picked = jnp.sum(jnp.where(chosen, logits[:, None, :], 0.0), axis=-1)
    picked_max = jnp.max(picked, axis=-1, keepdims=True)
    picked_exp = jnp.exp(picked - picked_max)
    gates = picked_exp / jnp.sum(picked_exp, axis=-1, keepdims=True)
    slot_dest = slot_index(routes.reshape(-1), experts, capacity)
    token_of = jnp.arange(tokens * topk, dtype=jnp.int32) // topk
    slot_token = jnp.full((experts * capacity,), -1, jnp.int32).at[slot_dest].set(token_of)
    filled = slot_token >= 0
    safe_token = jnp.maximum(slot_token, 0)
    gate_slot = jnp.zeros((experts * capacity,), jnp.float32).at[slot_dest].set(gates.reshape(-1))
    send_mid = jnp.where(filled[:, None], mid_low[safe_token], jnp.zeros((), jnp.bfloat16)).reshape(
        experts, capacity, width
    )
    send_grad = (
        (gate_slot[:, None] * out_grad[safe_token].astype(jnp.float32))
        .astype(jnp.bfloat16)
        .reshape(experts, capacity, width)
    )
    recv_mid, recv_grad = (
        lax.all_to_all(send_mid, ("shard", "ctx"), split_axis=0, concat_axis=1, tiled=True),
        lax.all_to_all(send_grad, ("shard", "ctx"), split_axis=0, concat_axis=1, tiled=True),
    )
    gate_up = jnp.einsum("erd,edjf->erjf", recv_mid, w_gate_up, preferred_element_type=jnp.float32)
    gate_val = gate_up[:, :, 0]
    up_val = gate_up[:, :, 1]
    gate_sig = jax.nn.sigmoid(gate_val)
    gate_act = gate_val * gate_sig
    hidden_act = (gate_act * up_val).astype(jnp.bfloat16)
    expert_part = jnp.einsum("erf,edf->erd", hidden_act, w_down, preferred_element_type=jnp.float32)
    hidden_grad = jnp.einsum("erd,edf->erf", recv_grad, w_down, preferred_element_type=jnp.float32)
    gate_grad = hidden_grad * up_val * gate_sig * (1.0 + gate_val * (1.0 - gate_sig))
    up_grad = hidden_grad * gate_act
    both_grad = jnp.stack([gate_grad, up_grad], axis=2).astype(jnp.bfloat16)
    mid_part = jnp.einsum(
        "erjf,edjf->erd", both_grad, w_gate_up, preferred_element_type=jnp.float32
    )
    gate_up_grad = jnp.einsum(
        "erd,erjf->edjf", recv_mid, both_grad, preferred_element_type=jnp.float32
    )
    down_grad = jnp.einsum(
        "erd,erf->edf", recv_grad, hidden_act, preferred_element_type=jnp.float32
    )
    out_grad_f = out_grad.astype(jnp.float32)
    back_rows, back_grads = (
        lax.all_to_all(expert_part, ("shard", "ctx"), split_axis=1, concat_axis=0, tiled=True),
        lax.all_to_all(mid_part, ("shard", "ctx"), split_axis=1, concat_axis=0, tiled=True),
    )
    columns = back_rows.shape[-1]
    rows_y = back_rows.reshape(experts * capacity, columns)[slot_dest].reshape(
        tokens, topk, columns
    )
    rows_g = back_grads.reshape(experts * capacity, columns)[slot_dest].reshape(
        tokens, topk, columns
    )
    mixture_part = jnp.sum(gates[:, :, None] * rows_y, axis=1)
    grad_part = jnp.sum(rows_g, axis=1)
    score_part = jnp.sum(out_grad_f[:, None, :] * rows_y, axis=2)
    mixture_part, grad_part, score_part = (mixture_part, grad_part, score_part)
    mixture, mid_grad, score_total = lax.psum((mixture_part, grad_part, score_part), "tp")
    output = (resid + mixture).astype(jnp.bfloat16)
    picked_grad = gates * (score_total - jnp.sum(gates * score_total, axis=1, keepdims=True))
    logit_grad = jnp.sum(jnp.where(chosen, picked_grad[:, :, None], 0.0), axis=1)
    router_grad = lax.dot_general(
        mid_norm, logit_grad, (((0,), (0,)), ((), ())), precision=lax.Precision.HIGHEST
    )
    mid_grad = mid_grad + lax.dot_general(
        logit_grad, router_f, (((1,), (1,)), ((), ())), precision=lax.Precision.HIGHEST
    )
    mid_scaled = gain_mid * mid_grad
    resid_grad = out_grad_f + rate_mid * (
        mid_scaled - mid_hat * jnp.mean(mid_hat * mid_scaled, axis=-1, keepdims=True)
    )
    gain_mid_grad = jnp.sum(mid_grad * mid_hat, axis=0)
    attn_low = resid_grad.astype(jnp.bfloat16)
    out_proj_grad = lax.dot_general(
        attn_low, mixed_low, (((0,), (0,)), ((), ())), preferred_element_type=jnp.float32
    )
    mixed_grad = (
        jnp.dot(attn_low, out_all, preferred_element_type=jnp.float32)
        .astype(jnp.bfloat16)
        .reshape(tokens, head_count, HEAD)
    )
    again = (
        jnp.einsum("qhd,khd->hqk", q_low, key_heads, preferred_element_type=jnp.float32)
        * score_scale
    )
    again = jnp.where(visible[None], again, masked_score)
    weights_again = jnp.exp(again - log_total)
    weights_low = weights_again.astype(jnp.bfloat16)
    weight_grad = jnp.einsum(
        "qhd,khd->hqk", mixed_grad, value_heads, preferred_element_type=jnp.float32
    )
    score_grad = weights_again * (
        weight_grad - jnp.sum(weights_again * weight_grad, axis=-1, keepdims=True)
    )
    score_low = score_grad.astype(jnp.bfloat16)
    q_grad = (
        jnp.einsum("hqk,khd->qhd", score_low, key_heads, preferred_element_type=jnp.float32)
        * score_scale
    )
    k_part = (
        jnp.einsum("hqk,qhd->khd", score_low, q_low, preferred_element_type=jnp.float32)
        * score_scale
    )
    v_part = jnp.einsum("hqk,qhd->khd", weights_low, mixed_grad, preferred_element_type=jnp.float32)
    k_grad, v_grad = (
        lax.psum_scatter(
            k_part.reshape(group_len, half_width), "ctx", scatter_dimension=0, tiled=True
        ),
        lax.psum_scatter(
            v_part.reshape(group_len, half_width), "ctx", scatter_dimension=0, tiled=True
        ),
    )
    q_in = rotate_back(q_grad, cosine, sine).reshape(tokens, half_width)
    k_in = rotate_back(k_grad.reshape(tokens, head_count, HEAD), cosine, sine).reshape(
        tokens, half_width
    )
    q_scaled = gain_q * q_in
    k_scaled = gain_k * k_in
    inner_q, inner_k = lax.psum(
        (jnp.sum(q_scaled * q_hat, axis=1), jnp.sum(k_scaled * k_hat, axis=1)), "tp"
    )
    q_raw_grad = rate_q * (q_scaled - q_hat * (inner_q / full_heads)[:, None])
    k_raw_grad = rate_k * (k_scaled - k_hat * (inner_k / full_heads)[:, None])
    gain_pair = jnp.stack([jnp.sum(q_in * q_hat, axis=0), jnp.sum(k_in * k_hat, axis=0)], axis=1)
    qk_gain_part = lax.dynamic_update_slice(
        jnp.zeros((width, 2), jnp.float32), gain_pair, (tp_index * half_width, 0)
    )
    raw_grad = jnp.stack([q_raw_grad, k_raw_grad, v_grad], axis=1).astype(jnp.bfloat16)
    qkv_grad = jnp.einsum(
        "td,tjh->jdh", in_low, raw_grad, preferred_element_type=jnp.float32
    ).reshape(3 * width, half_width)
    norm_part = jnp.einsum("tjh,jdh->td", raw_grad, qkv_mats, preferred_element_type=jnp.float32)
    in_norm_grad, qk_gain_grad = (
        lax.psum(norm_part.astype(jnp.bfloat16), "tp").astype(jnp.float32),
        lax.psum(qk_gain_part.astype(jnp.bfloat16), "tp").astype(jnp.float32),
    )
    in_scaled = gain_in * in_norm_grad
    input_grad = resid_grad + rate_in * (
        in_scaled - in_hat * jnp.mean(in_hat * in_scaled, axis=-1, keepdims=True)
    )
    gain_in_grad = jnp.sum(in_norm_grad * in_hat, axis=0)
    gains_grad = jnp.stack(
        [gain_in_grad, gain_mid_grad, qk_gain_grad[:, 0], qk_gain_grad[:, 1]], axis=1
    )
    qkv_owned, out_owned, gains_owned, router_owned = (
        lax.psum_scatter(qkv_grad, ("shard", "ctx"), scatter_dimension=0, tiled=True),
        lax.psum_scatter(out_proj_grad, ("shard", "ctx"), scatter_dimension=0, tiled=True),
        lax.psum_scatter(gains_grad, ("shard", "ctx"), scatter_dimension=0, tiled=True),
        lax.psum_scatter(router_grad, ("shard", "ctx"), scatter_dimension=0, tiled=True),
    )
    return (
        output,
        input_grad,
        qkv_owned,
        out_owned,
        gains_owned,
        router_owned,
        gate_up_grad,
        down_grad,
    )


def solution(mesh):
    in_specs = (
        P(("shard", "ctx"), None),
        P(("shard", "ctx"), "tp"),
        P(("shard", "ctx"), "tp"),
        P(("shard", "ctx"), None),
        P(("shard", "ctx"), None),
        P(("shard", "ctx"), None, None, "tp"),
        P(("shard", "ctx"), None, "tp"),
        P(("shard", "ctx"), None),
        P("shard", None),
        P("shard", None),
        P(("shard", "ctx"), None),
    )
    out_specs = (
        P(("shard", "ctx"), None),
        P(("shard", "ctx"), None),
        P(("shard", "ctx"), "tp"),
        P(("shard", "ctx"), "tp"),
        P(("shard", "ctx"), None),
        P(("shard", "ctx"), None),
        P(("shard", "ctx"), None, None, "tp"),
        P(("shard", "ctx"), None, "tp"),
    )
    return jax.shard_map(local, mesh=mesh, in_specs=in_specs, out_specs=out_specs, check_vma=False)
```

profile of v0, /device:TPU:0, one launch (start us, length us, event | category | flops | bytes accessed | tf_op | source)
XLA Modules:
  0.0 2155.8 jit_solution(1457848799466026686)
XLA Ops:
  10.4 23.8 %all_gather.18 = bf16[2048,4]{0,1:T(4,128)(2,1)S(1)} all-gather(bf16[128,4]{0,1:T(4,128)(2,1)} %param.14), channel_id=1, replica_groups=mesh['shard'=4,'ctx'=4,'tp'=2] {'shard','ctx'}, dimensions={0}, use_global_device_ids=true | all-gather | bytes 17408 | tf_op jit(solution)/shard_map/all_gather | solution.py:75
  37.0 76.5 %all-gather.6.cloned.1.call-done = bf16[6144,1024]{1,0:T(8,128)(2,1)} async-done(((bf16[384,1024]{1,0:T(8,128)(2,1)}), bf16[6144,1024]{1,0:T(8,128)(2,1)}) %all-gather.6.cloned.1.call-update) | async-done | bytes 12582928 | tf_op jit(solution)/shard_map/all_gather | solution.py:73
  113.5 6.1 fusion.78
  143.6 18.0 all-gather.8.cloned.1.call-done
  168.4 45.7 %all-gather.10.cloned.1.call-done = bf16[2048,1024]{1,0:T(8,128)(2,1)} async-done(((bf16[128,1024]{1,0:T(8,128)(2,1)}), bf16[2048,1024]{1,0:T(8,128)(2,1)}) %all-gather.10.cloned.1.call-update) | async-done | bytes 4194320 | tf_op jit(solution)/shard_map/all_gather | solution.py:74
  224.9 6.4 scatter_custom_fusion
  231.5 37.7 %all-reduce.7.cloned.1.call-done = f32[192,2048]{1,0:T(8,128)} async-done(((f32[192,2048]{1,0:T(8,128)}), f32[192,2048]{1,0:T(8,128)}) %all-reduce.7.cloned.1.call-update) | async-done | bytes 1572880 | tf_op jit(solution)/shard_map/psum | solution.py:147
  272.2 8.6 gather_fusion
  280.9 7.1 broadcast_select_fusion
  288.0 5.8 all-to-all-start
  293.8 8.7 gather_fusion.2
  302.5 134.7 %all_gather.23 = bf16[2048,16]{0,1:T(8,128)(2,1)S(1)} all-gather(bf16[128,16]{0,1:T(8,128)(2,1)S(1)} %copy-done.70), channel_id=1, replica_groups=mesh['shard'=4,'ctx'=4,'tp'=2] {'shard','ctx'}, dimensions={0}, use_global_device_ids=true | all-gather | bytes 69632 | tf_op jit(solution)/shard_map/all_gather | solution.py:76
  441.7 6.2 scatter_custom_fusion.1
  448.0 7.7 fusion
  455.7 42.1 %all-to-all-start.2 = ((bf16[16,120,2048]{2,1,0:T(8,128)(2,1)}), bf16[16,120,2048]{2,1,0:T(8,128)(2,1)}, u32[]{:S(2)}, u32[]{:S(2)}) async-start(bf16[16,120,2048]{2,1,0:T(8,128)(2,1)} %fusion), calls=%async_computation.2 | async-start | bytes 15728640 | tf_op jit(solution)/shard_map/all_to_all | solution.py:176
  497.8 13.8 convolution_bitcast_fusion.4
  511.6 127.7 %all-to-all-done.2 = bf16[16,120,2048]{2,1,0:T(8,128)(2,1)} async-done(((bf16[16,120,2048]{2,1,0:T(8,128)(2,1)}), bf16[16,120,2048]{2,1,0:T(8,128)(2,1)}, u32[]{:S(2)}, u32[]{:S(2)}) %all-to-all-start.2) | async-done | bytes 7864352 | tf_op jit(solution)/shard_map/all_to_all | solution.py:176
  639.3 12.0 fusion.31
  651.3 10.6 convolution_bitcast_fusion
  662.0 22.7 %copy.137 = f32[1,1920,2048]{2,0,1:T(1,128)} copy(f32[1,1920,2048]{2,1,0:T(8,128)S(1)} %convolution_bitcast_fusion) | data formatting | bytes 31457280 | tf_op jit(solution)/shard_map/erjf,edjf->erd/dot_general | solution.py:189
  684.6 35.3 %all-to-all-start.3 = ((f32[1,1920,2048]{2,0,1:T(1,128)}), f32[1,1920,2048]{2,0,1:T(1,128)}, u32[]{:S(2)}, u32[]{:S(2)}) async-start(f32[1,1920,2048]{2,0,1:T(1,128)} %copy.137), calls=%async_computation.3 | async-start | bytes 31457280 | tf_op jit(solution)/shard_map/all_to_all | solution.py:201
  728.8 22.6 %copy.134 = f32[1,1920,2048]{2,0,1:T(1,128)} copy(f32[1,1920,2048]{2,1,0:T(8,128)S(1)} %convolution_bitcast_fusion.1) | data formatting | bytes 31457280 | tf_op jit(solution)/shard_map/erf,edf->erd/dot_general | solution.py:184
  751.5 246.8 %all-to-all-done.3 = f32[1,1920,2048]{2,0,1:T(1,128)} async-done(((f32[1,1920,2048]{2,0,1:T(1,128)}), f32[1,1920,2048]{2,0,1:T(1,128)}, u32[]{:S(2)}, u32[]{:S(2)}) %all-to-all-start.3) | async-done | bytes 15728672 | tf_op jit(solution)/shard_map/all_to_all | solution.py:201
  998.3 66.0 %all-to-all-start.1 = ((f32[1,1920,2048]{2,0,1:T(1,128)}), f32[1,1920,2048]{2,0,1:T(1,128)}, u32[]{:S(2)}, u32[]{:S(2)}) async-start(f32[1,1920,2048]{2,0,1:T(1,128)} %copy.134), calls=%async_computation.1 | async-start | bytes 31457280 | tf_op jit(solution)/shard_map/all_to_all | solution.py:200
  1064.8 18.7 copy.240
  1083.5 18.4 gather_fusion.3
  1101.9 8.7 bitcast_reduce_fusion
  1110.6 232.1 %all-to-all-done.1 = f32[1,1920,2048]{2,0,1:T(1,128)} async-done(((f32[1,1920,2048]{2,0,1:T(1,128)}), f32[1,1920,2048]{2,0,1:T(1,128)}, u32[]{:S(2)}, u32[]{:S(2)}) %all-to-all-start.1) | async-done | bytes 15728672 | tf_op jit(solution)/shard_map/all_to_all | solution.py:200
  1342.7 18.9 copy.241
  1361.6 18.2 gather_fusion.1
  1379.8 8.6 fusion.2
  1389.1 5.1 psum.75
  1394.3 140.6 %all-reduce.11.cloned.1.call-done = (f32[192,2048]{1,0:T(8,128)}, f32[192,2048]{1,0:T(8,128)}) async-done(((f32[192,2048]{1,0:T(8,128)}, f32[192,2048]{1,0:T(8,128)}), (f32[192,2048]{1,0:T(8,128)}, f32[192,2048]{1,0:T(8,128)})) %all-reduce.11.cloned.1.call-update) | async-done | bytes 3145744 | tf_op jit(solution)/shard_map/psum | solution.py:214
  1552.7 5.0 fusion.21
  1568.6 22.1 %reduce-scatter.9.cloned.1.call-done = f32[192,1024]{1,0:T(8,128)} async-done(((f32[768,1024]{1,0:T(8,128)}), f32[192,1024]{1,0:T(8,128)}) %reduce-scatter.9.cloned.1.call-update) | async-done | bytes 786448 | tf_op jit(solution)/shard_map/reduce_scatter | solution.py:262
  1594.8 5.0 all-reduce
  1602.9 28.7 %reduce-scatter.11.cloned.1.call-done = f32[192,1024]{1,0:T(8,128)} async-done(((f32[768,1024]{1,0:T(8,128)}), f32[192,1024]{1,0:T(8,128)}) %reduce-scatter.11.cloned.1.call-update) | async-done | bytes 786448 | tf_op jit(solution)/shard_map/reduce_scatter | solution.py:265
  1633.6 9.8 fusion.16
  1648.5 29.4 %all-reduce.9.cloned.1.call-done = bf16[192,2048]{1,0:T(8,128)(2,1)} async-done(((bf16[192,2048]{1,0:T(8,128)(2,1)}), bf16[192,2048]{1,0:T(8,128)(2,1)}) %all-reduce.9.cloned.1.call-update) | async-done | bytes 786448 | tf_op jit(solution)/shard_map/psum | solution.py:290
  1683.1 5.9 fusion.81
  1690.1 10.4 convolution_bitcast_fusion.2
  1700.5 24.7 %copy.148 = f32[3,2048,1024]{2,1,0:T(8,128)} copy(f32[3,2048,1024]{1,2,0:T(8,128)} %convolution_bitcast_fusion.2) | data formatting | bytes 50331648 | tf_op jit(solution)/shard_map/td,tjh->jdh/transpose | solution.py:285
  1726.8 12.1 convolution_bitcast_fusion.3
  1738.9 16.5 copy.150
  1755.4 9.6 convolution_bitcast_fusion.5
  1768.2 25.7 %reduce-scatter.17.cloned.1.call-done = f32[128,16]{0,1:T(8,128)} async-done(((f32[2048,16]{0,1:T(8,128)}), f32[128,16]{0,1:T(8,128)}) %reduce-scatter.17.cloned.1.call-update) | async-done | bytes 8208 | tf_op jit(solution)/shard_map/reduce_scatter | solution.py:305
  1793.9 107.1 %reduce-scatter.15.cloned.1.call-done = f32[128,1024]{1,0:T(8,128)} async-done(((f32[2048,1024]{1,0:T(8,128)}), f32[128,1024]{1,0:T(8,128)}) %reduce-scatter.15.cloned.1.call-update) | async-done | bytes 524304 | tf_op jit(solution)/shard_map/reduce_scatter | solution.py:303
  1900.9 247.9 %reduce-scatter.13.cloned.1.call-done = f32[384,1024]{1,0:T(8,128)} async-done(((f32[6144,1024]{1,0:T(8,128)}), f32[384,1024]{1,0:T(8,128)}) %reduce-scatter.13.cloned.1.call-update) | async-done | bytes 1572880 | tf_op jit(solution)/shard_map/reduce_scatter | solution.py:302
  (287 shorter events, 118.5 us)
Async XLA Ops:
  7.2 632.1 %copy-start = (bf16[1,2048,512]{2,1,0:T(8,128)(2,1)S(1)}, bf16[1,2048,512]{2,1,0:T(8,128)(2,1)}, u32[]{:S(2)}) copy-start(bf16[1,2048,512]{2,1,0:T(8,128)(2,1)} %param.17) | copy-start | bytes 6291460
  7.2 106.3 %copy-start.7 = (bf16[192,2048]{1,0:T(8,128)(2,1)S(1)}, bf16[192,2048]{1,0:T(8,128)(2,1)}, u32[]{:S(2)}) copy-start(bf16[192,2048]{1,0:T(8,128)(2,1)} %param.11) | copy-start | bytes 2359300
  7.2 106.3 %all-gather.6.cloned.1.call-start = ((), (), s32[]{:S(2)}) async-start(), calls=%async_computation.10 | async-start | bytes 13369344 | tf_op jit(solution)/shard_map/all_gather | solution.py:73
  7.9 132.7 %all-gather.12.cloned.1.call-start = ((), (), s32[]{:S(2)}) async-start(), calls=%async_computation.20 | async-start | bytes 1966080 | tf_op jit(solution)/shard_map/all_gather | solution.py:123
  35.5 99.5 %copy-start.35 = (f32[192,128]{1,0:T(8,128)}, f32[192,128]{1,0:T(8,128)S(1)}, u32[]{:S(2)}) copy-start(f32[192,128]{1,0:T(8,128)S(1)} %get-tuple-element.88) | copy-start | bytes 294916
  37.0 82.6 %copy-start.55 = (f32[192]{0:T(256)}, f32[192]{0:T(256)S(1)}, u32[]{:S(2)}) copy-start(f32[192]{0:T(256)S(1)} %add_rsqrt_fusion.3) | copy-start | bytes 2308
  37.0 82.6 %copy-start.39 = (f32[2048,1]{0,1:T(1,128)}, f32[2048,1]{0,1:T(1,128)S(1)}, u32[]{:S(2)}) copy-start(f32[2048,1]{0,1:T(1,128)S(1)} %get-tuple-element.94) | copy-start | bytes 24580
  37.0 400.2 %copy-start.43 = (f32[2048,1]{0,1:T(1,128)}, f32[2048,1]{0,1:T(1,128)S(1)}, u32[]{:S(2)}) copy-start(f32[2048,1]{0,1:T(1,128)S(1)} %get-tuple-element.91) | copy-start | bytes 24580
  121.8 39.8 %all-gather.8.cloned.1.call-start = ((), (), s32[]{:S(2)}) async-start(), calls=%async_computation.11 | async-start | bytes 1966080 | tf_op jit(solution)/shard_map/all_gather | solution.py:122
  121.9 13.2 copy-start.49
  121.9 14.6 copy-start.51
  136.4 25.2 %copy-start.19 = (bf16[192,8,128]{2,0,1:T(8,128)(2,1)}, bf16[192,8,128]{2,0,1:T(8,128)(2,1)S(1)}, u32[]{:S(2)}) copy-start(bf16[192,8,128]{2,0,1:T(8,128)(2,1)S(1)} %get-tuple-element.90) | copy-start | bytes 1179652
  139.6 74.4 %all-gather.10.cloned.1.call-start = ((), (), s32[]{:S(2)}) async-start(), calls=%async_computation.12 | async-start | bytes 4456448 | tf_op jit(solution)/shard_map/all_gather | solution.py:74
  140.2 129.0 %all-reduce.7.cloned.1.call-start = ((), (), s32[]{:S(2)}) async-start(), calls=%async_computation.13 | async-start | bytes 3145728 | tf_op jit(solution)/shard_map/psum | solution.py:147
  168.4 50.6 %copy-start.27 = (bf16[8,24,8,128]{3,2,1,0:T(8,128)(2,1)}, bf16[8,24,8,128]{3,2,1,0:T(8,128)(2,1)S(1)}, u32[]{:S(2)}) copy-start(bf16[8,24,8,128]{3,2,1,0:T(8,128)(2,1)S(1)} %fusion.57) | copy-start | bytes 1179652
  168.4 50.6 %copy-start.47 = (s32[192,8]{0,1:T(8,128)S(1)}, s32[192,8]{0,1:T(8,128)}, u32[]{:S(2)}) copy-start(s32[192,8]{0,1:T(8,128)} %param.18) | copy-start | bytes 18436
  270.9 166.3 %copy-start.57 = (f32[192]{0:T(256)}, f32[192]{0:T(256)S(1)}, u32[]{:S(2)}) copy-start(f32[192]{0:T(256)S(1)} %add_rsqrt_fusion) | copy-start | bytes 2308
  288.0 167.8 %all-to-all-start = ((bf16[16,120,2048]{2,1,0:T(8,128)(2,1)}), bf16[16,120,2048]{2,1,0:T(8,128)(2,1)}, u32[]{:S(2)}, u32[]{:S(2)}) async-start(bf16[16,120,2048]{2,1,0:T(8,128)(2,1)} %broadcast_select_fusion), calls=%async_computation | async-start | bytes 15728640 | tf_op jit(solution)/shard_map/all_to_all | solution.py:175
  441.6 14.1 copy-start.33
  455.7 183.6 %all-to-all-start.2 = ((bf16[16,120,2048]{2,1,0:T(8,128)(2,1)}), bf16[16,120,2048]{2,1,0:T(8,128)(2,1)}, u32[]{:S(2)}, u32[]{:S(2)}) async-start(bf16[16,120,2048]{2,1,0:T(8,128)(2,1)} %fusion), calls=%async_computation.2 | async-start | bytes 15728640 | tf_op jit(solution)/shard_map/all_to_all | solution.py:176
  639.3 12.0 copy-start.71
  684.6 313.6 %all-to-all-start.3 = ((f32[1,1920,2048]{2,0,1:T(1,128)}), f32[1,1920,2048]{2,0,1:T(1,128)}, u32[]{:S(2)}, u32[]{:S(2)}) async-start(f32[1,1920,2048]{2,0,1:T(1,128)} %copy.137), calls=%async_computation.3 | async-start | bytes 31457280 | tf_op jit(solution)/shard_map/all_to_all | solution.py:201
  998.3 344.4 %all-to-all-start.1 = ((f32[1,1920,2048]{2,0,1:T(1,128)}), f32[1,1920,2048]{2,0,1:T(1,128)}, u32[]{:S(2)}, u32[]{:S(2)}) async-start(f32[1,1920,2048]{2,0,1:T(1,128)} %copy.134), calls=%async_computation.1 | async-start | bytes 31457280 | tf_op jit(solution)/shard_map/all_to_all | solution.py:200
  1064.3 470.5 %all-reduce.11.cloned.1.call-start = ((), (), s32[]{:S(2)}) async-start(), calls=%async_computation.22 | async-start | bytes 6291456 | tf_op jit(solution)/shard_map/psum | solution.py:214
  1361.6 18.2 copy-start.34
  1388.4 146.5 %copy-start.6 = (f32[192,2048]{1,0:T(8,128)S(1)}, f32[192,2048]{1,0:T(8,128)}, u32[]{:S(2)}) copy-start(f32[192,2048]{1,0:T(8,128)} %copy-done.5) | copy-start | bytes 4718596
  1388.4 146.5 %copy-start.38 = (bf16[2048,16]{0,1:T(8,128)(2,1)S(1)}, bf16[2048,16]{0,1:T(8,128)(2,1)}, u32[]{:S(2)}) copy-start(bf16[2048,16]{0,1:T(8,128)(2,1)} %copy-done.37) | copy-start | bytes 196612
  1388.4 146.5 %copy-start.44 = (f32[2048,1]{0,1:T(1,128)S(1)}, f32[2048,1]{0,1:T(1,128)}, u32[]{:S(2)}) copy-start(f32[2048,1]{0,1:T(1,128)} %copy-done.43) | copy-start | bytes 24580
  1388.4 146.4 %copy-start.58 = (f32[192]{0:T(256)S(1)}, f32[192]{0:T(256)}, u32[]{:S(2)}) copy-start(f32[192]{0:T(256)} %copy-done.57) | copy-start | bytes 2308
  1388.5 202.2 %reduce-scatter.9.cloned.1.call-start = ((), (), s32[]{:S(2)}) async-start(), calls=%async_computation.14 | async-start | bytes 3932160 | tf_op jit(solution)/shard_map/reduce_scatter | solution.py:262
  1552.6 79.0 %reduce-scatter.11.cloned.1.call-start = ((), (), s32[]{:S(2)}) async-start(), calls=%async_computation.15 | async-start | bytes 3932160 | tf_op jit(solution)/shard_map/reduce_scatter | solution.py:265
  1561.4 116.6 %all-reduce.9.cloned.1.call-start = ((), (), s32[]{:S(2)}) async-start(), calls=%async_computation.16 | async-start | bytes 1572864 | tf_op jit(solution)/shard_map/psum | solution.py:290
  1567.1 23.5 %copy-start.36 = (f32[192,128]{1,0:T(8,128)S(1)}, f32[192,128]{1,0:T(8,128)}, u32[]{:S(2)}) copy-start(f32[192,128]{1,0:T(8,128)} %copy-done.35) | copy-start | bytes 294916
  1568.6 23.6 %copy-start.16 = (f32[192,8,128]{2,1,0:T(8,128)S(1)}, f32[192,8,128]{2,1,0:T(8,128)}, u32[]{:S(2)}) copy-start(f32[192,8,128]{2,1,0:T(8,128)} %copy-done.15) | copy-start | bytes 2359300
  1568.6 23.6 %copy-start.52 = (f32[1024,1]{0,1:T(1,128)S(1)}, f32[1024,1]{0,1:T(1,128)}, u32[]{:S(2)}) copy-start(f32[1024,1]{0,1:T(1,128)} %copy-done.51) | copy-start | bytes 12292
  1568.6 23.6 %copy-start.62 = (f32[192]{0:T(256)S(1)}, f32[192]{0:T(256)}, u32[]{:S(2)}) copy-start(f32[192]{0:T(256)} %copy-done.61) | copy-start | bytes 2308
  1602.9 40.5 %copy-start.29 = (bf16[192,1,1024]{2,0,1:T(8,128)(2,1)}, bf16[192,1,1024]{2,0,1:T(8,128)(2,1)S(1)}, u32[]{:S(2)}) copy-start(bf16[192,1,1024]{2,0,1:T(8,128)(2,1)S(1)} %multiply_convert_fusion.4) | copy-start | bytes 1179652
  1633.6 44.4 %copy-start.8 = (bf16[192,2048]{1,0:T(8,128)(2,1)S(1)}, bf16[192,2048]{1,0:T(8,128)(2,1)}, u32[]{:S(2)}) copy-start(bf16[192,2048]{1,0:T(8,128)(2,1)} %param.11) | copy-start | bytes 2359300
  1633.6 44.4 %copy-start.40 = (f32[2048,1]{0,1:T(1,128)S(1)}, f32[2048,1]{0,1:T(1,128)}, u32[]{:S(2)}) copy-start(f32[2048,1]{0,1:T(1,128)} %copy-done.39) | copy-start | bytes 24580
  1633.6 44.4 %copy-start.56 = (f32[192]{0:T(256)S(1)}, f32[192]{0:T(256)}, u32[]{:S(2)}) copy-start(f32[192]{0:T(256)} %copy-done.55) | copy-start | bytes 2308
  1643.4 123.3 %reduce-scatter.19.cloned.1.call-start = ((), (), s32[]{:S(2)}) async-start(), calls=%async_computation.21 | async-start | bytes 1114112
  1681.2 112.7 %reduce-scatter.17.cloned.1.call-start = ((), (), s32[]{:S(2)}) async-start(), calls=%async_computation.19 | async-start | bytes 139264 | tf_op jit(solution)/shard_map/reduce_scatter | solution.py:305
  1683.0 217.9 %reduce-scatter.15.cloned.1.call-start = ((), (), s32[]{:S(2)}) async-start(), calls=%async_computation.18 | async-start | bytes 8912896 | tf_op jit(solution)/shard_map/reduce_scatter | solution.py:303
  1689.1 459.8 %reduce-scatter.13.cloned.1.call-start = ((), (), s32[]{:S(2)}) async-start(), calls=%async_computation.17 | async-start | bytes 26738688 | tf_op jit(solution)/shard_map/reduce_scatter | solution.py:302
  1738.9 16.5 copy-start.25
  1755.4 9.6 copy-start.10
  1755.4 9.7 copy-start.22
  1765.1 383.7 %copy-start.1 = (bf16[1,2048,512]{2,1,0:T(8,128)(2,1)S(1)}, bf16[1,2048,512]{2,1,0:T(8,128)(2,1)}, u32[]{:S(2)}) copy-start(bf16[1,2048,512]{2,1,0:T(8,128)(2,1)} %param.17) | copy-start | bytes 6291460
  (44 other events, 114.2 us)
Sparse Core Ops, SparseCore 0:
  10.3 103.1 all-gather.5
  121.9 17.8 all-gather.11
  142.0 19.6 all-gather.7
  163.7 50.3 all-gather.9
  219.1 50.0 all-reduce.6
  1388.6 146.2 all-reduce.10
  1552.7 37.8 reduce-scatter.8
  1593.7 37.8 reduce-scatter.10
  1643.5 34.3 all-reduce.8
  1681.4 57.5 reduce-scatter.18
  1743.0 50.8 reduce-scatter.16
  1798.4 102.5 reduce-scatter.14
  1905.6 243.1 reduce-scatter.12
where the time goes:
time: 2170 us; the launch traced here: 2160 us
  waiting for transfers between devices  1390 us (64%)
  local copies, waits for them, and re-layouts  224 us (10%)
  blocking collectives  179 us (8%)
  starting transfers between devices  150 us (7%)
  matrix products  126 us (6%)
  other arithmetic  74.3 us (3%)
    reduce_scatter x1, waiting for transfers between devices, local(): lax.psum_scatter(qkv_grad, ('shard', 'ctx'), scatter_dimension=0, tiled=T...  248 us
    all_to_all x1, waiting for transfers between devices, local(): lax.all_to_all(mid_part, ('shard', 'ctx'), split_axis=1, concat_axis=0, t...  247 us
    all_to_all x1, waiting for transfers between devices, local(): lax.all_to_all(expert_part, ('shard', 'ctx'), split_axis=1, concat_axis=0...  232 us
    psum x1, waiting for transfers between devices, local(): lax.psum((mixture_part, grad_part, score_part), 'tp')  141 us
    all_gather x1, blocking collectives, local(): lax.all_gather(router, ('shard', 'ctx'), axis=0, tiled=True)  135 us
    all_to_all x1, waiting for transfers between devices, local(): lax.all_to_all(send_grad, ('shard', 'ctx'), split_axis=0, concat_axis=1,...  128 us
    reduce_scatter x1, waiting for transfers between devices, local(): lax.psum_scatter(out_proj_grad, ('shard', 'ctx'), scatter_dimension=0, ti...  107 us
    unnamed x159, local copies, waits for them, and re-layouts  76.6 us
  transfers between devices with their start and end apart: 17, of which 14 were waited for; matrix products, arithmetic and copies ran while one was open for 12% of the time, Pallas kernels for 0%

commit v1 on v0

v1 whole, which is shorter than its diff:
```python
import jax
import jax.numpy as jnp
from jax import lax
from jax.sharding import PartitionSpec as P

HEAD = 128
LANES = 128


norm_eps = 1e-05
rope_base = 10000.0
masked_score = -1e30


def places_info(order_row, length_row):
    seq_ends = jnp.cumsum(length_row)
    seq_starts = seq_ends - length_row
    sequence = jnp.sum((order_row[:, None] >= seq_ends[None, :]).astype(jnp.int32), axis=1)
    picker = jnp.arange(length_row.shape[0], dtype=jnp.int32)[None, :] == sequence[:, None]
    first_place = jnp.sum(jnp.where(picker, seq_starts[None, :], 0), axis=1)
    return (sequence, order_row - first_place)


def rope_tables(place_pos, head_size):
    freq_index = jnp.arange(head_size // 2, dtype=jnp.float32)
    inverse = 1.0 / rope_base ** (freq_index * 2.0 / head_size)
    angle = place_pos.astype(jnp.float32)[:, None] * inverse[None, :]
    cosine = jnp.cos(angle)
    sine = jnp.sin(angle)
    return (jnp.concatenate([cosine, cosine], 1), jnp.concatenate([sine, sine], 1))


def rotate(values_in, cosine, sine):
    half_width = values_in.shape[-1] // 2
    turned = jnp.concatenate([-values_in[..., half_width:], values_in[..., :half_width]], -1)
    return values_in * cosine[:, None, :] + turned * sine[:, None, :]


def rotate_back(grad_in, cosine, sine):
    half_width = grad_in.shape[-1] // 2
    scaled = grad_in * sine[:, None, :]
    return grad_in * cosine[:, None, :] + jnp.concatenate(
        [scaled[..., half_width:], -scaled[..., :half_width]], -1
    )


def swap_tp(values_in):
    return lax.ppermute(values_in, "tp", [(0, 1), (1, 0)])


def swap_ctx(values_in, bit):
    return lax.ppermute(values_in, "ctx", [(i, i ^ bit) for i in range(lax.axis_size("ctx"))])


def join_halves(mine, other, first_is_mine):
    top = jnp.where(first_is_mine, mine, other)
    bottom = jnp.where(first_is_mine, other, mine)
    return jnp.concatenate([top, bottom], axis=0)


def split_three(values_in):
    high = values_in.astype(jnp.bfloat16)
    rest = values_in - high.astype(jnp.float32)
    middle = rest.astype(jnp.bfloat16)
    low = (rest - middle.astype(jnp.float32)).astype(jnp.bfloat16)
    return [high, middle, low]


def local(
    layer_in,
    w_qkv,
    w_out,
    norm_gains,
    router,
    w_gate_up,
    w_down,
    routes,
    lengths,
    token_order,
    out_grad,
):
    bf16, f32 = jnp.bfloat16, jnp.float32
    highest = lax.Precision.HIGHEST
    tokens, width = layer_in.shape
    experts = router.shape[1]
    hidden = w_down.shape[2]
    half = tokens // 2
    owners = ("shard", "ctx")
    tp_index = lax.axis_index("tp")
    ctx_index = lax.axis_index("ctx")
    ctx_size = lax.axis_size("ctx")
    expert_index = lax.axis_index("shard") * ctx_size + ctx_index
    first_is_mine = tp_index == 0
    my_row = tp_index * half
    other_row = (1 - tp_index) * half

    def my_rows(values_in):
        return lax.dynamic_slice_in_dim(values_in, my_row, half)

    def other_rows(values_in):
        return lax.dynamic_slice_in_dim(values_in, other_row, half)

    small_all = lax.all_gather(
        jnp.concatenate([norm_gains, router], axis=1), owners, axis=0, tiled=True
    )
    qkv_all = lax.all_gather(w_qkv, owners, axis=0, tiled=True)
    out_all = lax.all_gather(w_out, owners, axis=0, tiled=True)
    grad_half = my_rows(out_grad)
    grad_rows = lax.all_gather(grad_half, owners, axis=0, tiled=True)
    gate_own = w_gate_up[0, :, 0]
    up_own = w_gate_up[0, :, 1]
    down_own = w_down[0]
    gate_other, up_other, down_other = swap_tp(gate_own), swap_tp(up_own), swap_tp(down_own)
    w_in = jnp.concatenate([gate_own, gate_other, up_own, up_other], axis=1)
    w_back = jnp.concatenate([down_own, down_other], axis=1)

    half_width = qkv_all.shape[1]
    full_heads = half_width * lax.axis_size("tp")
    head_count = half_width // HEAD
    gains_f = small_all[:, :4].astype(f32)
    router_f = small_all[:, 4:].astype(f32)
    gain_in = gains_f[:, 0]
    gain_mid = gains_f[:, 1]
    gain_q = lax.dynamic_slice_in_dim(gains_f[:, 2], tp_index * half_width, half_width)
    gain_k = lax.dynamic_slice_in_dim(gains_f[:, 3], tp_index * half_width, half_width)
    score_scale = HEAD ** (-0.5)
    seq_all, pos_all = places_info(token_order[0], lengths[0])

    def ctx_rows(table, index):
        return lax.dynamic_slice_in_dim(table, index * tokens, tokens)

    seq_mine, pos_mine = ctx_rows(seq_all, ctx_index), ctx_rows(pos_all, ctx_index)
    key_order = [ctx_index ^ step for step in range(ctx_size)]
    seq_keys = jnp.concatenate([ctx_rows(seq_all, i) for i in key_order])
    pos_keys = jnp.concatenate([ctx_rows(pos_all, i) for i in key_order])
    cosine, sine = rope_tables(pos_mine, HEAD)
    visible = (seq_mine[:, None] == seq_keys[None, :]) & (pos_keys[None, :] <= pos_mine[:, None])

    layer_f = layer_in.astype(f32)
    rate_in = lax.rsqrt(jnp.mean(layer_f * layer_f, axis=-1, keepdims=True) + norm_eps)
    in_hat = layer_f * rate_in
    in_low = (in_hat * gain_in).astype(bf16)
    qkv_mats = qkv_all.reshape(3, width, half_width)
    q_raw, k_raw, v_raw = (
        jnp.dot(in_low, qkv_mats[j], preferred_element_type=f32) for j in range(3)
    )
    square_q, square_k = lax.psum(
        (jnp.sum(q_raw * q_raw, axis=1), jnp.sum(k_raw * k_raw, axis=1)), "tp"
    )
    rate_q = lax.rsqrt(square_q / full_heads + norm_eps)[:, None]
    rate_k = lax.rsqrt(square_k / full_heads + norm_eps)[:, None]
    q_hat = q_raw * rate_q
    k_hat = k_raw * rate_k
    q_low = rotate((q_hat * gain_q).reshape(tokens, head_count, HEAD), cosine, sine).astype(bf16)
    k_low = (
        rotate((k_hat * gain_k).reshape(tokens, head_count, HEAD), cosine, sine)
        .astype(bf16)
        .reshape(tokens, half_width)
    )
    v_low = v_raw.astype(bf16)

    def gather_ctx(block):
        far = swap_ctx(block, 2)
        return jnp.concatenate([block, swap_ctx(block, 1), far, swap_ctx(far, 1)], axis=0)

    group_len = tokens * ctx_size
    key_heads = gather_ctx(k_low).reshape(group_len, head_count, HEAD)
    value_heads = gather_ctx(v_low).reshape(group_len, head_count, HEAD)
    scores = jnp.einsum("qhd,khd->hqk", q_low, key_heads, preferred_element_type=f32) * score_scale
    scores = jnp.where(visible[None], scores, masked_score)
    row_max = jnp.max(scores, axis=-1, keepdims=True)
    shifted = jnp.exp(scores - row_max)
    row_sum = jnp.sum(shifted, axis=-1, keepdims=True)
    weights = shifted / row_sum
    log_total = row_max + jnp.log(row_sum)
    mixed = jnp.einsum(
        "hqk,khd->qhd", weights.astype(bf16), value_heads, preferred_element_type=f32
    )
    mixed_low = mixed.reshape(tokens, half_width).astype(bf16)
    attn_part = lax.dot_general(
        mixed_low, out_all, (((1,), (1,)), ((), ())), preferred_element_type=f32
    )
    attn = my_rows(attn_part) + swap_tp(other_rows(attn_part).astype(bf16)).astype(f32)

    resid = my_rows(layer_f) + attn
    rate_mid = lax.rsqrt(jnp.mean(resid * resid, axis=-1, keepdims=True) + norm_eps)
    mid_hat = resid * rate_mid
    mid_norm = mid_hat * gain_mid
    logits = jnp.dot(mid_norm, router_f, precision=highest)
    expert_ids = jnp.arange(experts, dtype=jnp.int32)
    chosen = jnp.any(my_rows(routes)[:, :, None] == expert_ids[None, None, :], axis=1)
    logits_max = jnp.max(jnp.where(chosen, logits, -jnp.inf), axis=-1, keepdims=True)
    gates = jnp.where(chosen, jnp.exp(jnp.where(chosen, logits - logits_max, 0.0)), 0.0)
    gates = gates / jnp.sum(gates, axis=-1, keepdims=True)

    def padded(parts):
        columns = sum(part.shape[1] for part in parts)
        rest = -columns % LANES
        if rest:
            parts = parts + [jnp.zeros((parts[0].shape[0], rest), parts[0].dtype)]
        return jnp.concatenate(parts, axis=1)

    mid_rows = lax.all_gather(
        padded([mid_norm.astype(bf16)] + split_three(gates)), owners, axis=0, tiled=True
    )
    extra = mid_rows[:, width:].astype(f32)
    column = jnp.arange(extra.shape[1], dtype=jnp.int32)
    mine_in = (column % experts == expert_index) & (column < 3 * experts)
    gate_col = jnp.sum(jnp.where(mine_in[None, :], extra, 0.0), axis=1, keepdims=True)
    mid_all = mid_rows[:, :width]

    hidden_raw = jnp.dot(grad_rows, w_back, preferred_element_type=f32)
    both = jnp.dot(mid_all, w_in, preferred_element_type=f32)
    gate_val, up_val = both[:, : 2 * hidden], both[:, 2 * hidden :]
    gate_sig = jax.nn.sigmoid(gate_val)
    gate_act = gate_val * gate_sig
    hidden_act = gate_act * up_val
    score_col = jnp.sum(hidden_act * hidden_raw, axis=1, keepdims=True)
    gated_act = (gate_col * hidden_act).astype(bf16)
    hidden_grad = gate_col * hidden_raw
    gate_grad = hidden_grad * up_val * gate_sig * (1.0 + gate_val * (1.0 - gate_sig))
    up_grad = hidden_grad * gate_act
    both_grad = jnp.concatenate([gate_grad.astype(bf16), up_grad.astype(bf16)], axis=1)
    mix_part = lax.dot_general(
        gated_act, w_back, (((1,), (1,)), ((), ())), preferred_element_type=f32
    ).astype(bf16)
    back_part = lax.dot_general(
        both_grad, w_in, (((1,), (1,)), ((), ())), preferred_element_type=f32
    ).astype(bf16)
    score_high = score_col.astype(bf16)
    score_low = (score_col - score_high.astype(f32)).astype(bf16)
    pads = -2 * experts % LANES + 2 * experts
    spot = jnp.arange(pads, dtype=jnp.int32)[None, :]
    zero = jnp.zeros((), bf16)
    score_part = jnp.where(
        spot == expert_index, score_high, jnp.where(spot == expert_index + experts, score_low, zero)
    )
    mix_sum = lax.psum_scatter(
        jnp.concatenate([mix_part, score_part], axis=1), owners, scatter_dimension=0, tiled=True
    )
    back_sum = lax.psum_scatter(back_part, owners, scatter_dimension=0, tiled=True)

    in_grad = lax.dot_general(
        mid_all, both_grad, (((0,), (0,)), ((), ())), preferred_element_type=f32
    )
    back_grad = lax.dot_general(
        grad_rows, gated_act, (((0,), (0,)), ((), ())), preferred_element_type=f32
    )

    def own_total(total, index):
        own = total[:, 2 * index * hidden : (2 * index + 1) * hidden]
        other = total[:, (2 * index + 1) * hidden : (2 * index + 2) * hidden]
        return own + swap_tp(other.astype(bf16)).astype(f32)

    gate_up_grad = jnp.stack([own_total(in_grad, 0), own_total(in_grad, 1)], axis=1)[None]
    down_grad = own_total(back_grad, 0)[None]

    mixture = mix_sum[:, :width].astype(f32)
    score_total = (
        mix_sum[:, width : width + experts].astype(f32)
        + mix_sum[:, width + experts : width + 2 * experts].astype(f32)
    )
    mid_grad = back_sum.astype(f32)
    output_half = (resid + mixture).astype(bf16)
    output = join_halves(output_half, swap_tp(output_half), first_is_mine)
    logit_grad = gates * (score_total - jnp.sum(gates * score_total, axis=1, keepdims=True))
    router_grad = lax.dot_general(
        logit_grad, mid_norm, (((0,), (0,)), ((), ())), precision=highest
    )
    mid_grad = mid_grad + lax.dot_general(
        logit_grad, router_f, (((1,), (1,)), ((), ())), precision=highest
    )
    mid_scaled = gain_mid * mid_grad
    resid_grad = grad_half.astype(f32) + rate_mid * (
        mid_scaled - mid_hat * jnp.mean(mid_hat * mid_scaled, axis=-1, keepdims=True)
    )
    gain_mid_grad = jnp.sum(mid_grad * mid_hat, axis=0, keepdims=True)
    attn_half = resid_grad.astype(bf16)
    attn_low = join_halves(attn_half, swap_tp(attn_half), first_is_mine)
    out_proj_grad = lax.dot_general(
        attn_low, mixed_low, (((0,), (0,)), ((), ())), preferred_element_type=f32
    ).astype(bf16)
    out_owned = lax.psum_scatter(
        out_proj_grad, owners, scatter_dimension=0, tiled=True
    ).astype(f32)
    mixed_grad = (
        jnp.dot(attn_low, out_all, preferred_element_type=f32)
        .astype(bf16)
        .reshape(tokens, head_count, HEAD)
    )
    again = jnp.einsum("qhd,khd->hqk", q_low, key_heads, preferred_element_type=f32) * score_scale
    again = jnp.where(visible[None], again, masked_score)
    weights_again = jnp.exp(again - log_total)
    weights_low = weights_again.astype(bf16)
    weight_grad = jnp.einsum("qhd,khd->hqk", mixed_grad, value_heads, preferred_element_type=f32)
    score_grad = weights_again * (
        weight_grad - jnp.sum(weights_again * weight_grad, axis=-1, keepdims=True)
    )
    score_low = score_grad.astype(bf16)
    q_grad = (
        jnp.einsum("hqk,khd->qhd", score_low, key_heads, preferred_element_type=f32) * score_scale
    )
    k_part = (
        jnp.einsum("hqk,qhd->khd", score_low, q_low, preferred_element_type=f32) * score_scale
    )
    v_part = jnp.einsum("hqk,qhd->khd", weights_low, mixed_grad, preferred_element_type=f32)

    def scatter_ctx(part):
        part = part.reshape(ctx_size, tokens, half_width)
        near = part[0] + swap_ctx(part[1].astype(bf16), 1).astype(f32)
        far = part[2] + swap_ctx(part[3].astype(bf16), 1).astype(f32)
        return near + swap_ctx(far.astype(bf16), 2).astype(f32)

    k_grad, v_grad = scatter_ctx(k_part), scatter_ctx(v_part)
    q_in = rotate_back(q_grad, cosine, sine).reshape(tokens, half_width)
    k_in = rotate_back(k_grad.reshape(tokens, head_count, HEAD), cosine, sine).reshape(
        tokens, half_width
    )
    q_scaled = gain_q * q_in
    k_scaled = gain_k * k_in
    inner_q, inner_k = lax.psum(
        (jnp.sum(q_scaled * q_hat, axis=1), jnp.sum(k_scaled * k_hat, axis=1)), "tp"
    )
    q_raw_grad = rate_q * (q_scaled - q_hat * (inner_q / full_heads)[:, None])
    k_raw_grad = rate_k * (k_scaled - k_hat * (inner_k / full_heads)[:, None])
    raw_grads = [q_raw_grad.astype(bf16), k_raw_grad.astype(bf16), v_grad.astype(bf16)]
    qkv_grad = jnp.concatenate(
        [
            lax.dot_general(
                in_low, raw, (((0,), (0,)), ((), ())), preferred_element_type=f32
            ).astype(bf16)
            for raw in raw_grads
        ],
        axis=0,
    )
    qkv_owned = lax.psum_scatter(qkv_grad, owners, scatter_dimension=0, tiled=True).astype(f32)
    norm_part = sum(
        lax.dot_general(raw, mat, (((1,), (1,)), ((), ())), preferred_element_type=f32)
        for raw, mat in zip(raw_grads, (qkv_mats[0], qkv_mats[1], qkv_mats[2]))
    )
    in_norm_grad = my_rows(norm_part) + swap_tp(other_rows(norm_part).astype(bf16)).astype(f32)
    in_hat_half = my_rows(in_hat)
    in_scaled = gain_in * in_norm_grad
    input_half = resid_grad + my_rows(rate_in) * (
        in_scaled - in_hat_half * jnp.mean(in_hat_half * in_scaled, axis=-1, keepdims=True)
    )
    input_grad = join_halves(input_half, swap_tp(input_half), first_is_mine)
    gain_in_grad = jnp.sum(in_norm_grad * in_hat_half, axis=0, keepdims=True)
    gain_pair = jnp.stack([jnp.sum(q_in * q_hat, axis=0), jnp.sum(k_in * k_hat, axis=0)], axis=0)
    qk_gain_part = lax.dynamic_update_slice(
        jnp.zeros((2, width), f32), gain_pair, (0, tp_index * half_width)
    )
    everyone = ("shard", "ctx", "tp")
    router_total = lax.psum(router_grad, everyone)
    gains_total = lax.psum(
        jnp.concatenate([gain_in_grad, gain_mid_grad, qk_gain_part], axis=0), everyone
    )
    own_rows = norm_gains.shape[0]

    def owned(total):
        return lax.dynamic_slice_in_dim(total, expert_index * own_rows, own_rows, axis=1).T

    return (
        output,
        input_grad,
        qkv_owned,
        out_owned,
        owned(gains_total),
        owned(router_total),
        gate_up_grad,
        down_grad,
    )


def solution(mesh):
    in_specs = (
        P(("shard", "ctx"), None),
        P(("shard", "ctx"), "tp"),
        P(("shard", "ctx"), "tp"),
        P(("shard", "ctx"), None),
        P(("shard", "ctx"), None),
        P(("shard", "ctx"), None, None, "tp"),
        P(("shard", "ctx"), None, "tp"),
        P(("shard", "ctx"), None),
        P("shard", None),
        P("shard", None),
        P(("shard", "ctx"), None),
    )
    out_specs = (
        P(("shard", "ctx"), None),
        P(("shard", "ctx"), None),
        P(("shard", "ctx"), "tp"),
        P(("shard", "ctx"), "tp"),
        P(("shard", "ctx"), None),
        P(("shard", "ctx"), None),
        P(("shard", "ctx"), None, None, "tp"),
        P(("shard", "ctx"), None, "tp"),
    )
    return jax.shard_map(local, mesh=mesh, in_specs=in_specs, out_specs=out_specs, check_vma=False)
```

time: 2170 us -> 922 us (0.42)
  waiting for transfers between devices: 1390 us -> 489 us
  local copies, waits for them, and re-layouts: 224 us -> 64.8 us
  starting transfers between devices: 150 us -> 19.3 us
  blocking collectives: 179 us -> 80.9 us
  matrix products: 126 us -> 159 us
    all_to_all x4 -> x0, waiting for transfers between devices: 607 us -> none  [the longest x1 247 us: local(): lax.all_to_all(mid_part, ('shard', 'ctx'), split_axis=1, concat_axis=0, t...]
    reduce_scatter x5 -> x4, waiting for transfers between devices: 431 us -> 153 us  [the longest x1 87.1 us: local(): lax.psum_scatter(back_part, owners, scatter_dimension=0, tiled=True)]
    ppermute x0 -> x23, waiting for transfers between devices: none -> 212 us  [the longest x11 184 us: swap_tp(): return lax.ppermute(values_in, 'tp', [(0, 1), (1, 0)])]
    psum x3 -> x1, waiting for transfers between devices: 208 us -> 0.01 us  [local(): router_total = lax.psum(router_grad, everyone)]
    all_to_all x4 -> x0, starting transfers between devices: 149 us -> none  [the longest x1 66 us: local(): lax.all_to_all(expert_part, ('shard', 'ctx'), split_axis=1, concat_axis=0...]
    all_gather x2 -> x1, blocking collectives: 159 us -> 24 us  [local(): lax.all_gather(jnp.concatenate([norm_gains, router], axis=1), owners, axi...]
    gather x4 -> x0, local copies, waits for them, and re-layouts: 54 us -> none  [the longest x1 18.4 us: local(): back_grads.reshape(experts * capacity, columns)[slot_dest]]
    unnamed x159 -> x150, local copies, waits for them, and re-layouts: 76.6 us -> 30.3 us
  transfers between devices with their start and end apart: 17 -> 32, of which waited for: 14 -> 16; matrix products, arithmetic and copies ran while one was open for 12% -> 28% of each run, Pallas kernels for 0% -> 0%
where the time goes in v1:
time: 922 us; the launch traced here: 918 us
  waiting for transfers between devices  489 us (53%)
  matrix products  159 us (17%)
  other arithmetic  88.7 us (10%)
  blocking collectives  80.9 us (9%)
  local copies, waits for them, and re-layouts  64.8 us (7%)
  starting transfers between devices  19.3 us (2%)
  between operations  15.2 us (2%)
    ppermute x11, waiting for transfers between devices, swap_tp(): return lax.ppermute(values_in, 'tp', [(0, 1), (1, 0)])  184 us
    reduce_scatter x1, waiting for transfers between devices, local(): lax.psum_scatter(back_part, owners, scatter_dimension=0, tiled=True)  87.1 us
    all_gather x1, waiting for transfers between devices, local(): qkv_all = lax.all_gather(w_qkv, owners, axis=0, tiled=True)  73.5 us
    reduce_scatter x1, waiting for transfers between devices, local(): lax.psum_scatter(jnp.concatenate([mix_part, score_part], axis=1), owners,...  65.8 us
    psum x1, blocking collectives, local(): lax.psum(jnp.concatenate([gain_in_grad, gain_mid_grad, qk_gain_part], axi...  46 us
    all_gather x1, waiting for transfers between devices, local(): lax.all_gather(padded([mid_norm.astype(bf16)] + split_three(gates)), owne...  44.3 us
    unnamed x150, local copies, waits for them, and re-layouts  30.3 us
    ppermute x12, waiting for transfers between devices, swap_ctx(): lax.ppermute(values_in, 'ctx', [(i, i ^ bit) for i in range(lax.axis_size...  27.9 us
  transfers between devices with their start and end apart: 32, of which 16 were waited for; matrix products, arithmetic and copies ran while one was open for 28% of the time, Pallas kernels for 0%

profile of v1, /device:TPU:0, one launch (start us, length us, event | category | flops | bytes accessed | tf_op | source)
XLA Modules:
  0.0 917.5 jit_solution(1776653212641304968)
XLA Ops:
  9.4 24.0 %all_gather.15 = bf16[2048,20]{0,1:T(8,128)(2,1)S(1)} all-gather(bf16[128,20]{0,1:T(8,128)(2,1)S(1)} %pad_maximum_fusion.19), channel_id=1, replica_groups=mesh['shard'=4,'ctx'=4,'tp'=2] {'shard','ctx'}, dimensions={0}, use_global_device_ids=true | all-gather | bytes 87040 | tf_op jit(solution)/shard_map/all_gather | solution.py:103
  40.1 73.5 %all-gather.5.cloned.1.call-done = bf16[6144,1024]{1,0:T(8,128)(2,1)} async-done(((bf16[384,1024]{1,0:T(8,128)(2,1)}), bf16[6144,1024]{1,0:T(8,128)(2,1)}) %all-gather.5.cloned.1.call-update) | async-done | bytes 12582928 | tf_op jit(solution)/shard_map/all_gather | solution.py:106
  113.6 3.6 multiply_reduce_fusion.11
  117.2 3.6 multiply_reduce_fusion.12
  120.9 5.1 all-reduce.1
  129.4 3.2 fusion.44
  135.3 5.5 collective-permute-done.4
  140.8 14.3 %collective-permute-done.1 = bf16[192,1024]{1,0:T(8,128)(2,1)S(1)} collective-permute-done((bf16[192,1024]{1,0:T(8,128)(2,1)S(1)}, bf16[192,1024]{1,0:T(8,128)(2,1)S(1)}, u32[]{:S(2)}, u32[]{:S(2)}) %collective-permute-start.1) | collective-permute-done | bytes 393248 | tf_op jit(solution)/shard_map/ppermute | solution.py:52
  164.8 5.3 all-gather.7.cloned.1.call-done
  170.1 3.7 fusion.69
  177.6 8.7 collective-permute-done.6
  191.9 9.1 fusion.103
  208.3 44.3 %all-gather.9.cloned.1.call-done = bf16[1536,2176]{1,0:T(8,128)(2,1)} async-done(((bf16[96,2176]{1,0:T(8,128)(2,1)}), bf16[1536,2176]{1,0:T(8,128)(2,1)}) %all-gather.9.cloned.1.call-update) | async-done | bytes 6684688 | tf_op jit(solution)/shard_map/all_gather | solution.py:203
  253.7 42.9 %collective-permute-done.7 = bf16[2048,512]{1,0:T(8,128)(2,1)} collective-permute-done((bf16[2048,512]{1,0:T(8,128)(2,1)}, bf16[2048,512]{1,0:T(8,128)(2,1)}, u32[]{:S(2)}, u32[]{:S(2)}) %collective-permute-start.7) | collective-permute-done | bytes 2097184 | tf_op jit(solution)/shard_map/ppermute | solution.py:48
  296.6 20.6 %fusion.3 = f32[1536,2048]{1,0:T(8,128)} fusion(bf16[1536,2176]{1,0:T(8,128)(2,1)} %all-gather.9.cloned.1.call-done, bf16[2048,512]{1,0:T(8,128)(2,1)} %collective-permute-done.8, bf16[2048,512]{1,0:T(8,128)(2,1)} %bitcast.181, bf16[2048,512]{1,0:T(8,128)(2,1)} %collective-permute-done.7, bf16[2048,512]{1,0:T(8,128)(2,1)} %bitcast.182), kind=kOutput, calls=%fused_computation.16 | convolution fusion | flops 12918456320 | bytes 27262976 | tf_op jit(solution)/shard_map/dot_general | solution.py:213
  317.3 22.8 %collective-permute-done.9 = bf16[2048,512]{1,0:T(8,128)(2,1)} collective-permute-done((bf16[2048,512]{1,0:T(8,128)(2,1)}, bf16[2048,512]{1,0:T(8,128)(2,1)}, u32[]{:S(2)}, u32[]{:S(2)}) %collective-permute-start.9) | collective-permute-done | bytes 2097184 | tf_op jit(solution)/shard_map/ppermute | solution.py:48
  340.0 15.8 %multiply_convert_fusion.1 = (bf16[1536,1024]{1,0:T(8,128)(2,1)}, bf16[1536,1024]{1,0:T(8,128)(2,1)}, f32[1536]{0:T(1024)S(1)}, bf16[1536,1024]{1,0:T(8,128)(2,1)S(1)}) fusion(f32[1536,2048]{1,0:T(8,128)} %fusion.3, f32[1536]{0:T(1024)S(1)} %select_reduce_fusion, bf16[1536,2048]{1,0:T(8,128)(2,1)} %all-gather.11.cloned.1.call-done, ...), kind=kOutput, calls=%fused_computation.8 | convolution fusion | flops 6480722432 | bytes 32518144 | tf_op jit(solution)/shard_map/dot_general | solution.py:212
  356.3 10.1 %convolution_convert_fusion.1 = bf16[1536,2048]{1,0:T(8,128)(2,1)S(1)} fusion(bf16[1536,1024]{1,0:T(8,128)(2,1)S(1)} %get-tuple-element.76, bf16[2048,512]{1,0:T(8,128)(2,1)} %collective-permute-done.9, bf16[2048,512]{1,0:T(8,128)(2,1)} %bitcast.11), kind=kOutput, calls=%fused_computation.4 | convolution fusion | flops 6453985280 | bytes 13631488 | tf_op jit(solution)/shard_map/dot_general | solution.py:224
  366.4 3.6 pad_maximum_fusion.2
  370.1 20.1 %convolution_convert_fusion = bf16[1536,2048]{1,0:T(8,128)(2,1)} fusion(bf16[1536,1024]{1,0:T(8,128)(2,1)} %get-tuple-element.72, bf16[1536,1024]{1,0:T(8,128)(2,1)} %get-tuple-element.71, bf16[2048,512]{1,0:T(8,128)(2,1)} %collective-permute-done.8, bf16[2048,512]{1,0:T(8,128)(2,1)} %bitcast.181, bf16[2048,512]{1,0:T(8,128)(2,1)} %collective-permute-done.7, ...), kind=kOutput, calls=%fused_computation.3 | convolution fusion | flops 12934184960 | bytes 20971520 | tf_op jit(solution)/shard_map/dot_general | solution.py:227
  390.3 65.8 %reduce-scatter.13.cloned.1.call-done = bf16[96,2176]{1,0:T(8,128)(2,1)} async-done(((bf16[1536,2176]{1,0:T(8,128)(2,1)}), bf16[96,2176]{1,0:T(8,128)(2,1)}) %reduce-scatter.13.cloned.1.call-update) | async-done | bytes 417808 | tf_op jit(solution)/shard_map/reduce_scatter | solution.py:238
  457.2 87.1 %reduce-scatter.15.cloned.1.call-done = bf16[96,2048]{1,0:T(8,128)(2,1)} async-done(((bf16[1536,2048]{1,0:T(8,128)(2,1)}), bf16[96,2048]{1,0:T(8,128)(2,1)}) %reduce-scatter.15.cloned.1.call-update) | async-done | bytes 393232 | tf_op jit(solution)/shard_map/reduce_scatter | solution.py:241
  553.3 6.2 collective-permute-done.11
  560.3 3.3 convolution_convert_fusion.2
  563.6 3.5 fusion.50
  567.1 3.4 multiply_reduce_fusion.1
  576.1 3.3 broadcast_multiply_fusion.1
  584.4 5.3 fusion.116
  593.5 2.7 fusion.104
  601.4 8.1 collective-permute-done.14
  611.0 3.2 multiply_reduce_fusion.3
  614.2 5.8 all-reduce
  630.6 25.7 %pad_maximum_fusion = bf16[6144,1024]{1,0:T(8,128)(2,1)} fusion(bf16[2048,1024]{1,0:T(8,128)(2,1)S(1)} %convolution_convert_fusion.3, bf16[2048,1024]{1,0:T(8,128)(2,1)S(1)} %convolution_convert_fusion.4, bf16[2048,1024]{1,0:T(8,128)(2,1)S(1)} %convolution_convert_fusion.5), kind=kLoop, calls=%fused_computation | loop fusion | flops 37748736 | bytes 25165824 | tf_op jit(solution)/shard_map/concatenate | solution.py:327
  656.4 10.1 %fusion.118 = f32[2048,1024]{1,0:T(8,128)S(1)} fusion(bf16[1536,2048]{1,0:T(8,128)(2,1)} %all-gather.11.cloned.1.call-done, bf16[1536,1024]{1,0:T(8,128)(2,1)} %copy-done.66), kind=kOutput, calls=%fused_computation.243 | convolution fusion | flops 6442450944 | bytes 17825792 | tf_op jit(solution)/shard_map/dot_general | solution.py:246
  666.4 3.3 copy-done.18
  673.0 21.8 %fusion.117 = (bf16[2048,2048]{1,0:T(8,128)(2,1)}, f32[2048,2048]{1,0:T(8,128)}) fusion(bf16[1536,1024]{1,0:T(8,128)(2,1)} %get-tuple-element.72, bf16[1536,1024]{1,0:T(8,128)(2,1)S(1)} %copy-done.67, bf16[1536,2176]{1,0:T(8,128)(2,1)} %all-gather.9.cloned.1.call-done), kind=kOutput, calls=%fused_computation.242 | convolution fusion | flops 12901679104 | bytes 37748736 | tf_op jit(solution)/shard_map/dot_general | solution.py:243
  694.7 4.7 fusion.102
  701.7 18.5 %collective-permute-done.22 = bf16[2048,512]{1,0:T(8,128)(2,1)} collective-permute-done((bf16[2048,512]{1,0:T(8,128)(2,1)}, bf16[2048,512]{1,0:T(8,128)(2,1)}, u32[]{:S(2)}, u32[]{:S(2)}) %collective-permute-start.22) | collective-permute-done | bytes 2097184 | tf_op jit(solution)/shard_map/ppermute | solution.py:48
  720.2 5.6 fusion.5
  725.8 39.4 %collective-permute-done.20 = bf16[2048,512]{1,0:T(8,128)(2,1)} collective-permute-done((bf16[2048,512]{1,0:T(8,128)(2,1)}, bf16[2048,512]{1,0:T(8,128)(2,1)}, u32[]{:S(2)}, u32[]{:S(2)}) %collective-permute-start.20) | collective-permute-done | bytes 2097184 | tf_op jit(solution)/shard_map/ppermute | solution.py:48
  765.2 41.7 %collective-permute-done.21 = bf16[2048,512]{1,0:T(8,128)(2,1)} collective-permute-done((bf16[2048,512]{1,0:T(8,128)(2,1)}, bf16[2048,512]{1,0:T(8,128)(2,1)}, u32[]{:S(2)}, u32[]{:S(2)}) %collective-permute-start.21) | collective-permute-done | bytes 2097184 | tf_op jit(solution)/shard_map/ppermute | solution.py:48
  806.9 6.2 fusion.7
  813.1 3.7 fusion.13
  816.8 3.8 fusion.23
  820.7 3.8 fusion.26
  827.7 16.5 %copy.184 = f32[1,2048,2,512]{3,2,1,0:T(2,128)} copy(f32[1,2048,2,512]{3,1,2,0:T(8,128)S(1)} %maximum_bitcast_fusion) | data formatting | bytes 16777216
  851.3 3.9 collective-permute-done.10
  857.3 46.0 %psum.46 = f32[4,2048]{1,0:T(4,128)S(1)} all-reduce(f32[4,2048]{1,0:T(4,128)S(1)} %pad_maximum_fusion.18), channel_id=1, replica_groups=mesh['shard'=4,'ctx'=4,'tp'=2] {'shard','ctx','tp'}, use_global_device_ids=true, to_apply=%region_32.33 | all-reduce | flops 8192 | bytes 65536 | tf_op jit(solution)/shard_map/psum | solution.py:355
  (311 shorter events, 110.2 us)
Async XLA Ops:
  7.2 170.3 %copy-start = (s32[192,8]{0,1:T(8,128)S(1)}, s32[192,8]{0,1:T(8,128)}, u32[]{:S(2)}) copy-start(s32[192,8]{0,1:T(8,128)} %param.18) | copy-start | bytes 18436
  7.2 106.4 %all-gather.5.cloned.1.call-start = ((), (), s32[]{:S(2)}) async-start(), calls=%async_computation.4 | async-start | bytes 13369344 | tf_op jit(solution)/shard_map/all_gather | solution.py:106
  7.9 162.2 %all-gather.7.cloned.1.call-start = ((), (), s32[]{:S(2)}) async-start(), calls=%async_computation.5 | async-start | bytes 4456448 | tf_op jit(solution)/shard_map/all_gather | solution.py:107
  8.7 243.9 %all-gather.9.cloned.1.call-start = ((), (), s32[]{:S(2)}) async-start(), calls=%async_computation.6 | async-start | bytes 7102464 | tf_op jit(solution)/shard_map/all_gather | solution.py:203
  36.7 92.7 %copy-start.23 = (f32[2048,1]{0,1:T(1,128)}, f32[2048,1]{0,1:T(1,128)S(1)}, u32[]{:S(2)}) copy-start(f32[2048,1]{0,1:T(1,128)S(1)} %get-tuple-element.115) | copy-start | bytes 24580
  36.8 90.6 %copy-start.45 = (f32[1024,1]{0,1:T(1,128)}, f32[1024,1]{0,1:T(1,128)S(1)}, u32[]{:S(2)}) copy-start(f32[1024,1]{0,1:T(1,128)S(1)} %get-tuple-element.151) | copy-start | bytes 12292
  36.8 91.2 %copy-start.43 = (f32[1024,1]{0,1:T(1,128)}, f32[1024,1]{0,1:T(1,128)S(1)}, u32[]{:S(2)}) copy-start(f32[1024,1]{0,1:T(1,128)S(1)} %get-tuple-element.150) | copy-start | bytes 12292
  38.0 89.4 %copy-start.26 = (f32[192,128]{1,0:T(8,128)}, f32[192,128]{1,0:T(8,128)S(1)}, u32[]{:S(2)}) copy-start(f32[192,128]{1,0:T(8,128)S(1)} %get-tuple-element.109) | copy-start | bytes 294916
  40.1 89.3 %copy-start.48 = (f32[192]{0:T(256)}, f32[192]{0:T(256)S(1)}, u32[]{:S(2)}) copy-start(f32[192]{0:T(256)S(1)} %add_rsqrt_fusion.2) | copy-start | bytes 2308
  128.8 26.3 %collective-permute-start.3 = (bf16[192,1024]{1,0:T(8,128)(2,1)S(1)}, bf16[192,1024]{1,0:T(8,128)(2,1)S(1)}, u32[]{:S(2)}, u32[]{:S(2)}) collective-permute-start(bf16[192,1024]{1,0:T(8,128)(2,1)S(1)} %fusion.55), channel_id=1, source_target_pairs={{0,2},{2,0},{4,6},{6,4},{1,3},{3,1},{5,7},{7,5},{8,10},{10,8},{12,... | collective-permute-start | bytes 1179656 | tf_op jit(solution)/shard_map/ppermute | solution.py:52
  128.8 12.0 %collective-permute-start.4 = (bf16[192,1024]{1,0:T(8,128)(2,1)S(1)}, bf16[192,1024]{1,0:T(8,128)(2,1)S(1)}, u32[]{:S(2)}, u32[]{:S(2)}) collective-permute-start(bf16[192,1024]{1,0:T(8,128)(2,1)S(1)} %fusion.55), channel_id=1, source_target_pairs={{0,4},{2,6},{4,0},{6,2},{1,5},{3,7},{5,1},{7,3},{8,12},{10,14},{12... | collective-permute-start | bytes 1179656 | tf_op jit(solution)/shard_map/ppermute | solution.py:52
  132.7 29.0 %copy-start.31 = (bf16[192,1024]{1,0:T(8,128)(2,1)}, bf16[192,1024]{1,0:T(8,128)(2,1)S(1)}, u32[]{:S(2)}) copy-start(bf16[192,1024]{1,0:T(8,128)(2,1)S(1)} %fusion.44) | copy-start | bytes 1179652
  132.7 22.5 %collective-permute-start.1 = (bf16[192,1024]{1,0:T(8,128)(2,1)S(1)}, bf16[192,1024]{1,0:T(8,128)(2,1)S(1)}, u32[]{:S(2)}, u32[]{:S(2)}) collective-permute-start(bf16[192,1024]{1,0:T(8,128)(2,1)S(1)} %fusion.44), channel_id=1, source_target_pairs={{0,4},{2,6},{4,0},{6,2},{1,5},{3,7},{5,1},{7,3},{8,12},{10,14},{12... | collective-permute-start | bytes 1179656 | tf_op jit(solution)/shard_map/ppermute | solution.py:52
  134.4 27.2 %collective-permute-start = (bf16[192,1024]{1,0:T(8,128)(2,1)S(1)}, bf16[192,1024]{1,0:T(8,128)(2,1)S(1)}, u32[]{:S(2)}, u32[]{:S(2)}) collective-permute-start(bf16[192,1024]{1,0:T(8,128)(2,1)S(1)} %fusion.44), channel_id=1, source_target_pairs={{0,2},{2,0},{4,6},{6,4},{1,3},{3,1},{5,7},{7,5},{8,10},{10,8},{12,... | collective-permute-start | bytes 1179656 | tf_op jit(solution)/shard_map/ppermute | solution.py:52
  140.8 16.0 %collective-permute-start.5 = (bf16[192,1024]{1,0:T(8,128)(2,1)S(1)}, bf16[192,1024]{1,0:T(8,128)(2,1)S(1)}, u32[]{:S(2)}, u32[]{:S(2)}) collective-permute-start(bf16[192,1024]{1,0:T(8,128)(2,1)S(1)} %collective-permute-done.4), channel_id=1, source_target_pairs={{0,2},{2,0},{4,6},{6,4},{1,3},{3,1},{5,7},{7,5},{8,10},{10,8},{12,... | collective-permute-start | bytes 1179656 | tf_op jit(solution)/shard_map/ppermute | solution.py:52
  155.1 6.5 collective-permute-start.2
  174.7 11.6 %collective-permute-start.6 = (bf16[96,2048]{1,0:T(8,128)(2,1)}, bf16[96,2048]{1,0:T(8,128)(2,1)}, u32[]{:S(2)}, u32[]{:S(2)}) collective-permute-start(bf16[96,2048]{1,0:T(8,128)(2,1)} %dynamic-slice_convert_fusion.1), channel_id=1, source_target_pairs={{0,1},{1,0},{2,3},{3,2},{4,5},{5,4},{6,7},{7,6},{8,9},{9,8},{10,11... | collective-permute-start | bytes 1179656 | tf_op jit(solution)/shard_map/ppermute | solution.py:48
  176.1 14.7 %copy-start.28 = (bf16[192,2048]{1,0:T(8,128)(2,1)S(1)}, bf16[192,2048]{1,0:T(8,128)(2,1)}, u32[]{:S(2)}) copy-start(bf16[192,2048]{1,0:T(8,128)(2,1)} %param.21) | copy-start | bytes 2359300
  187.8 356.5 %copy-start.62 = (f32[96]{0:T(128)}, f32[96]{0:T(128)S(1)}, u32[]{:S(2)}) copy-start(f32[96]{0:T(128)S(1)} %add_rsqrt_fusion.3) | copy-start | bytes 1156
  190.7 149.3 %all-gather.11.cloned.1.call-start = ((), (), s32[]{:S(2)}) async-start(), calls=%async_computation.7 | async-start | bytes 6684672 | tf_op jit(solution)/shard_map/all_gather | solution.py:109
  191.6 264.5 %reduce-scatter.13.cloned.1.call-start = ((), (), s32[]{:S(2)}) async-start(), calls=%async_computation.11 | async-start | bytes 7102464 | tf_op jit(solution)/shard_map/reduce_scatter | solution.py:238
  202.9 50.8 %collective-permute-start.8 = (bf16[2048,512]{1,0:T(8,128)(2,1)}, bf16[2048,512]{1,0:T(8,128)(2,1)}, u32[]{:S(2)}, u32[]{:S(2)}) collective-permute-start(bf16[2048,512]{1,0:T(8,128)(2,1)} %bitcast.181), channel_id=1, source_target_pairs={{0,1},{1,0},{2,3},{3,2},{4,5},{5,4},{6,7},{7,6},{8,9},{9,8},{10,11... | collective-permute-start | bytes 6291464 | tf_op jit(solution)/shard_map/ppermute | solution.py:48
  206.2 90.4 %collective-permute-start.7 = (bf16[2048,512]{1,0:T(8,128)(2,1)}, bf16[2048,512]{1,0:T(8,128)(2,1)}, u32[]{:S(2)}, u32[]{:S(2)}) collective-permute-start(bf16[2048,512]{1,0:T(8,128)(2,1)} %bitcast.182), channel_id=1, source_target_pairs={{0,1},{1,0},{2,3},{3,2},{4,5},{5,4},{6,7},{7,6},{8,9},{9,8},{10,11... | collective-permute-start | bytes 6291464 | tf_op jit(solution)/shard_map/ppermute | solution.py:48
  206.8 133.2 %collective-permute-start.9 = (bf16[2048,512]{1,0:T(8,128)(2,1)}, bf16[2048,512]{1,0:T(8,128)(2,1)}, u32[]{:S(2)}, u32[]{:S(2)}) collective-permute-start(bf16[2048,512]{1,0:T(8,128)(2,1)} %bitcast.11), channel_id=1, source_target_pairs={{0,1},{1,0},{2,3},{3,2},{4,5},{5,4},{6,7},{7,6},{8,9},{9,8},{10,11... | collective-permute-start | bytes 6291464 | tf_op jit(solution)/shard_map/ppermute | solution.py:48
  370.0 174.2 %reduce-scatter.15.cloned.1.call-start = ((), (), s32[]{:S(2)}) async-start(), calls=%async_computation.12 | async-start | bytes 6684672 | tf_op jit(solution)/shard_map/reduce_scatter | solution.py:241
  390.2 154.0 %copy-start.30 = (bf16[2048,20]{0,1:T(8,128)(2,1)S(1)}, bf16[2048,20]{0,1:T(8,128)(2,1)}, u32[]{:S(2)}) copy-start(bf16[2048,20]{0,1:T(8,128)(2,1)} %copy-done.29) | copy-start | bytes 245764
  390.2 454.5 %all-reduce.4.cloned.1.call-start = ((), (), s32[]{:S(2)}) async-start(), calls=%async_computation.10 | async-start | bytes 262144 | tf_op jit(solution)/shard_map/psum | solution.py:354
  457.0 89.5 %copy-start.50 = (bf16[96,16]{0,1:T(8,128)(2,1)}, bf16[96,16]{0,1:T(8,128)(2,1)S(1)}, u32[]{:S(2)}) copy-start(bf16[96,16]{0,1:T(8,128)(2,1)S(1)} %copy.199) | copy-start | bytes 9220
  457.1 89.4 %copy-start.52 = (bf16[96,16]{0,1:T(8,128)(2,1)}, bf16[96,16]{0,1:T(8,128)(2,1)S(1)}, u32[]{:S(2)}) copy-start(bf16[96,16]{0,1:T(8,128)(2,1)S(1)} %copy.198) | copy-start | bytes 9220
  457.2 89.4 %copy-start.64 = (f32[96]{0:T(128)}, f32[96]{0:T(128)S(1)}, u32[]{:S(2)}) copy-start(f32[96]{0:T(128)S(1)} %multiply_reduce_fusion.13) | copy-start | bytes 1156
  457.2 103.1 %copy-start.40 = (bf16[8,24,8,128]{3,2,1,0:T(8,128)(2,1)S(1)}, bf16[8,24,8,128]{3,2,1,0:T(8,128)(2,1)}, u32[]{:S(2)}) copy-start(bf16[8,24,8,128]{3,2,1,0:T(8,128)(2,1)} %copy-done.39) | copy-start | bytes 1179652
  549.2 10.3 %collective-permute-start.11 = (bf16[96,2048]{1,0:T(8,128)(2,1)S(1)}, bf16[96,2048]{1,0:T(8,128)(2,1)S(1)}, u32[]{:S(2)}, u32[]{:S(2)}) collective-permute-start(bf16[96,2048]{1,0:T(8,128)(2,1)S(1)} %get-tuple-element.61), channel_id=1, source_target_pairs={{0,1},{1,0},{2,3},{3,2},{4,5},{5,4},{6,7},{7,6},{8,9},{9,8},{10,11... | collective-permute-start | bytes 1179656 | tf_op jit(solution)/shard_map/ppermute | solution.py:48
  553.2 353.3 %reduce-scatter.11.cloned.1.call-start = ((), (), s32[]{:S(2)}) async-start(), calls=%async_computation.9 | async-start | bytes 4456448 | tf_op jit(solution)/shard_map/reduce_scatter | solution.py:283
  576.1 25.3 %collective-permute-start.12 = (bf16[192,1024]{1,0:T(8,128)(2,1)}, bf16[192,1024]{1,0:T(8,128)(2,1)}, u32[]{:S(2)}, u32[]{:S(2)}) collective-permute-start(bf16[192,1024]{1,0:T(8,128)(2,1)} %copy.187), channel_id=1, source_target_pairs={{0,2},{2,0},{4,6},{6,4},{1,3},{3,1},{5,7},{7,5},{8,10},{10,8},{12,... | collective-permute-start | bytes 1179656 | tf_op jit(solution)/shard_map/ppermute | solution.py:52
  582.8 13.3 %collective-permute-start.13 = (bf16[192,1024]{1,0:T(8,128)(2,1)}, bf16[192,1024]{1,0:T(8,128)(2,1)}, u32[]{:S(2)}, u32[]{:S(2)}) collective-permute-start(bf16[192,1024]{1,0:T(8,128)(2,1)} %copy.189), channel_id=1, source_target_pairs={{0,2},{2,0},{4,6},{6,4},{1,3},{3,1},{5,7},{7,5},{8,10},{10,8},{12,... | collective-permute-start | bytes 1179656 | tf_op jit(solution)/shard_map/ppermute | solution.py:52
  583.2 325.2 %reduce-scatter.9.cloned.1.call-start = ((), (), s32[]{:S(2)}) async-start(), calls=%async_computation.8 | async-start | bytes 13369344 | tf_op jit(solution)/shard_map/reduce_scatter | solution.py:336
  584.4 14.3 %copy-start.12 = (f32[192,8,64]{2,0,1:T(8,128)}, f32[192,8,64]{2,0,1:T(8,128)S(1)}, u32[]{:S(2)}) copy-start(f32[192,8,64]{2,0,1:T(8,128)S(1)} %get-tuple-element.91) | copy-start | bytes 1179652
  592.9 6.9 collective-permute-start.16
  593.1 31.0 %collective-permute-start.15 = (bf16[192,1024]{0,1:T(8,128)(2,1)}, bf16[192,1024]{0,1:T(8,128)(2,1)}, u32[]{:S(2)}, u32[]{:S(2)}) collective-permute-start(bf16[192,1024]{0,1:T(8,128)(2,1)} %bitcast.200), channel_id=1, source_target_pairs={{0,2},{2,0},{4,6},{6,4},{1,3},{3,1},{5,7},{7,5},{8,10},{10,8},{12,... | collective-permute-start | bytes 1179656 | tf_op jit(solution)/shard_map/ppermute | solution.py:52
  597.3 12.2 %collective-permute-start.14 = (bf16[192,1024]{1,0:T(8,128)(2,1)S(1)}, bf16[192,1024]{1,0:T(8,128)(2,1)S(1)}, u32[]{:S(2)}, u32[]{:S(2)}) collective-permute-start(bf16[192,1024]{1,0:T(8,128)(2,1)S(1)} %add_convert_fusion), channel_id=1, source_target_pairs={{0,4},{2,6},{4,0},{6,2},{1,5},{3,7},{5,1},{7,3},{8,12},{10,14},{12... | collective-permute-start | bytes 1179656 | tf_op jit(solution)/shard_map/ppermute | solution.py:52
  600.8 23.4 %collective-permute-start.17 = (bf16[192,1024]{0,1:T(8,128)(2,1)}, bf16[192,1024]{0,1:T(8,128)(2,1)}, u32[]{:S(2)}, u32[]{:S(2)}) collective-permute-start(bf16[192,1024]{0,1:T(8,128)(2,1)} %fusion.51), channel_id=1, source_target_pairs={{0,4},{2,6},{4,0},{6,2},{1,5},{3,7},{5,1},{7,3},{8,12},{10,14},{12... | collective-permute-start | bytes 1179656 | tf_op jit(solution)/shard_map/ppermute | solution.py:52
  671.4 48.8 %collective-permute-start.22 = (bf16[2048,512]{1,0:T(8,128)(2,1)}, bf16[2048,512]{1,0:T(8,128)(2,1)}, u32[]{:S(2)}, u32[]{:S(2)}) collective-permute-start(bf16[2048,512]{1,0:T(8,128)(2,1)} %slice.275), channel_id=1, source_target_pairs={{0,1},{1,0},{2,3},{3,2},{4,5},{5,4},{6,7},{7,6},{8,9},{9,8},{10,11... | collective-permute-start | bytes 6291464 | tf_op jit(solution)/shard_map/ppermute | solution.py:48
  699.5 65.7 %collective-permute-start.20 = (bf16[2048,512]{1,0:T(8,128)(2,1)}, bf16[2048,512]{1,0:T(8,128)(2,1)}, u32[]{:S(2)}, u32[]{:S(2)}) collective-permute-start(bf16[2048,512]{1,0:T(8,128)(2,1)} %get-tuple-element.77), channel_id=1, source_target_pairs={{0,1},{1,0},{2,3},{3,2},{4,5},{5,4},{6,7},{7,6},{8,9},{9,8},{10,11... | collective-permute-start | bytes 6291464 | tf_op jit(solution)/shard_map/ppermute | solution.py:48
  700.4 106.5 %collective-permute-start.21 = (bf16[2048,512]{1,0:T(8,128)(2,1)}, bf16[2048,512]{1,0:T(8,128)(2,1)}, u32[]{:S(2)}, u32[]{:S(2)}) collective-permute-start(bf16[2048,512]{1,0:T(8,128)(2,1)} %get-tuple-element.78), channel_id=1, source_target_pairs={{0,1},{1,0},{2,3},{3,2},{4,5},{5,4},{6,7},{7,6},{8,9},{9,8},{10,11... | collective-permute-start | bytes 6291464 | tf_op jit(solution)/shard_map/ppermute | solution.py:48
  825.2 20.8 %collective-permute-start.18 = (bf16[96,2048]{1,0:T(8,128)(2,1)}, bf16[96,2048]{1,0:T(8,128)(2,1)}, u32[]{:S(2)}, u32[]{:S(2)}) collective-permute-start(bf16[96,2048]{1,0:T(8,128)(2,1)} %dynamic-slice_convert_fusion), channel_id=1, source_target_pairs={{0,1},{1,0},{2,3},{3,2},{4,5},{5,4},{6,7},{7,6},{8,9},{9,8},{10,11... | collective-permute-start | bytes 1179656 | tf_op jit(solution)/shard_map/ppermute | solution.py:48
  827.7 16.5 %copy-start.22 = (bf16[96,2048]{1,0:T(8,128)(2,1)S(1)}, bf16[96,2048]{1,0:T(8,128)(2,1)}, u32[]{:S(2)}) copy-start(bf16[96,2048]{1,0:T(8,128)(2,1)} %get-tuple-element.97) | copy-start | bytes 1179652
  844.2 10.9 %collective-permute-start.10 = (bf16[96,2048]{1,0:T(8,128)(2,1)S(1)}, bf16[96,2048]{1,0:T(8,128)(2,1)}, u32[]{:S(2)}, u32[]{:S(2)}) collective-permute-start(bf16[96,2048]{1,0:T(8,128)(2,1)S(1)} %copy-done.22), channel_id=1, source_target_pairs={{0,1},{1,0},{2,3},{3,2},{4,5},{5,4},{6,7},{7,6},{8,9},{9,8},{10,11... | collective-permute-start | bytes 1179656 | tf_op jit(solution)/shard_map/ppermute | solution.py:48
  849.8 54.1 %collective-permute-start.19 = (f32[96,2048]{1,0:T(8,128)}, f32[96,2048]{1,0:T(8,128)S(1)}, u32[]{:S(2)}, u32[]{:S(2)}) collective-permute-start(f32[96,2048]{1,0:T(8,128)} %multiply_add_fusion), channel_id=1, source_target_pairs={{0,1},{1,0},{2,3},{3,2},{4,5},{5,4},{6,7},{7,6},{8,9},{9,8},{10,11... | collective-permute-start | bytes 2359304 | tf_op jit(solution)/shard_map/ppermute | solution.py:48
  (54 other events, 322.0 us)
Sparse Core Ops, SparseCore 0:
  10.3 103.2 all-gather.4
  115.7 54.3 all-gather.6
  190.9 61.6 all-gather.8
  255.3 60.1 all-gather.10
  370.2 85.8 reduce-scatter.12
  459.9 84.3 reduce-scatter.14
  553.4 122.7 all-reduce.3
  680.1 71.7 reduce-scatter.10
  755.9 134.6 reduce-scatter.8
